TPU v7x, 32 devices: a whole 2x2x4 slice. The times are simulated.
32 devices in a mesh: space: 16 (over z, x, core), sample: 2 (over y).
Axes of the slice: x: 2, y: 2, z: 4, core: 2. Of those that a mesh axis runs over, the one named last changes fastest.
Arguments:
- spectra: float32 [36, 2, 512, 256], P('sample', None, 'space'), may hold values from -6 to 6
- plane_assign: int32 [2, 18], P('sample'), may hold values from 0 to 17, each once within a row
- fine_state: bfloat16 [4, 32, 131072], P('sample', 'space'), may hold values from 0.3984375 to 1.3984375
- partner_state: float32 [4, 4, 2048], P('sample'), may hold values from 0.4 to 1.4
- coarse_state: float32 [32, 4, 2048], P(('space', 'sample')), may hold values from 0.4 to 1.4
- turbine_x: int32 [16], replicated, may hold values from 0 to 31
- turbine_y: int32 [16], replicated, may hold values from 0 to 62
- turbine_z: int32 [16], replicated, may hold values from 0 to 30
- thrust: float32 [16], replicated, may hold values from 0.5 to 2
Outputs:
- fine_field: float32 [4, 32, 131072], P('sample', 'space')
- partner_field: float32 [4, 4, 2048], P('sample')
- coarse_field: float32 [32, 4, 2048], P(('space', 'sample'))
- estimate: float32 [2], replicated
Inputs may be any that keep to these rules, and one draw needn't show every extreme that they name: `plane_assign`: each row is a permutation of 0 to 17.
All inputs are finite; a program needn't handle non-finite values.
Results may differ from a plain program's by a relative error of at most 0.0003.
Values sent between devices are 32-bit elements; how exact they have to be, the bound alone decides.
A program may use at most 128 MiB of HBM per device.

v0:
```python
import math
import jax
import jax.numpy as jnp
from jax import lax
from jax.sharding import PartitionSpec as P

STEPS = 2
ADVECT = 0.3
DIFFUSE = 0.1
RELAX = 0.05
AMPLITUDE = 0.2
HIGHEST = lax.Precision.HIGHEST


def with_halo(cells, sides, width):
    for axis, dim in sides:
        count = lax.axis_size(axis)
        ends = count - 1
        head = lax.slice_in_dim(cells, 0, width, axis=dim)
        tail = lax.slice_in_dim(cells, cells.shape[dim] - width, cells.shape[dim], axis=dim)
        cells = jnp.concatenate(
            [
                lax.ppermute(tail, axis, [(i, (i + 1) % count) for i in range(ends)]),
                cells,
                lax.ppermute(head, axis, [((i + 1) % count, i) for i in range(ends)]),
            ],
            axis=dim,
        )
    return cells


def advance(extended, inflow, resistance):
    upstream = extended[..., :-2, :, :]
    centre = extended[..., 1:-1, :, :]
    downstream = extended[..., 2:, :, :]
    lateral = (
        jnp.roll(centre, 1, -2)
        + jnp.roll(centre, -1, -2)
        + jnp.roll(centre, 1, -1)
        + jnp.roll(centre, -1, -1)
        - 4.0 * centre
    )
    updated = (
        centre
        + ADVECT * (upstream - centre)
        + DIFFUSE * (upstream + downstream - 2.0 * centre)
        + DIFFUSE * lateral
        + RELAX * (inflow[..., None, :, :] - centre)
    )
    return updated / (1.0 + resistance)


def drag_field(
    turbine_x, turbine_y, turbine_z, thrust, first_plane, length, factor, y_count, z_count
):
    block_size = 8 // factor
    planes = first_plane + jnp.arange(length, dtype=jnp.int32)
    along_x = jnp.where(
        (turbine_x // factor)[:, None] == planes[None, :],
        thrust[:, None],
        jnp.zeros_like(thrust)[:, None],
    )
    y_index = jnp.arange(y_count, dtype=jnp.int32)
    z_index = jnp.arange(z_count, dtype=jnp.int32)
    low_y = (turbine_y * block_size)[:, None]
    low_z = (turbine_z * block_size)[:, None]
    cover_y = ((y_index[None, :] >= low_y) & (y_index[None, :] < low_y + 2 * block_size)).astype(
        thrust.dtype
    )
    cover_z = ((z_index[None, :] >= low_z) & (z_index[None, :] < low_z + 2 * block_size)).astype(
        thrust.dtype
    )
    cross_mask = (cover_y[:, :, None] * cover_z[:, None, :]).reshape(
        thrust.shape[0], y_count * z_count
    )
    return jnp.dot(along_x.T, cross_mask, precision=HIGHEST).reshape(length, y_count, z_count)


def restrict(values):
    leading = values.shape[:-2]
    y_count = values.shape[-2]
    z_count = values.shape[-1]
    return values.reshape(leading + (y_count // 8, 8, z_count // 8, 8)).mean(axis=(-3, -1))


def run_whole(velocity, inflow, resistance):
    for step_index in range(STEPS):
        extended = jnp.concatenate(
            [inflow[..., None, :, :], velocity, velocity[..., -1:, :, :]], axis=-3
        )
        velocity = advance(extended, inflow, resistance)
    return velocity


def twiddle(first_index, second_index, period):
    turn_count = first_index[:, None] * second_index[None, :] % period
    phases = 2.0 * math.pi / period * turn_count.astype(jnp.float32)
    return (jnp.cos(phases), jnp.sin(phases))


def shards(
    spectra,
    plane_assign,
    fine_state,
    partner_state,
    coarse_state,
    turbine_x,
    turbine_y,
    turbine_z,
    thrust,
):
    spaces = lax.axis_size("space")
    slab_index = lax.axis_index("space")
    ky_rows = spectra.shape[2]
    total_y = ky_rows * spaces
    total_z = spectra.shape[3]
    coarse_y = total_y // 8
    coarse_z = total_z // 8
    pair_count = fine_state.shape[0]
    slab_planes = fine_state.shape[1]
    norm_scale = 1.0 / math.sqrt(total_y * total_z)
    assignment = plane_assign[0]
    pair_spectra = jnp.take(spectra, assignment[:pair_count], axis=0)
    alone_spectra = jnp.take(spectra, assignment[pair_count:], axis=0)
    z_cells = jnp.arange(total_z, dtype=jnp.int32)
    y_cells = jnp.arange(total_y, dtype=jnp.int32)
    cosine_z, sine_z = twiddle(z_cells, z_cells, total_z)
    z_table = jnp.stack(
        [jnp.concatenate([cosine_z, sine_z], axis=1), jnp.concatenate([-sine_z, cosine_z], axis=1)]
    )
    cosine_y, sine_y = twiddle(y_cells, y_cells, total_y)
    y_table = jnp.stack([cosine_y, -sine_y])
    pair_pq = jnp.einsum("ncks,csj->nkj", pair_spectra, z_table, precision=HIGHEST).reshape(
        pair_count, ky_rows, 2, total_z
    )
    own_ky = slab_index * ky_rows + jnp.arange(ky_rows, dtype=jnp.int32)
    cosine_own, sine_own = twiddle(own_ky, y_cells, total_y)
    y_own = jnp.stack([cosine_own, -sine_own])
    partial_noise = jnp.einsum("nkcz,cky->nyz", pair_pq, y_own, precision=HIGHEST)
    fine_noise = lax.psum(partial_noise, "space") * norm_scale
    alone_pq = jnp.einsum("ncks,csj->nkj", alone_spectra, z_table, precision=HIGHEST)
    gathered_pq = lax.all_to_all(alone_pq, "space", split_axis=0, concat_axis=1, tiled=True)
    full_plane = jnp.einsum(
        "nkcz,cky->nyz", gathered_pq.reshape(-1, total_y, 2, total_z), y_table, precision=HIGHEST
    )
    alone_noise = restrict(full_plane * norm_scale)
    fine_inflow = 1.0 + AMPLITUDE * fine_noise
    last_plane = slab_planes * spaces - 1
    slab_start = slab_index * slab_planes
    velocity = fine_state.astype(jnp.float32).reshape(pair_count, slab_planes, total_y, total_z)
    fine_drag = drag_field(
        turbine_x, turbine_y, turbine_z, thrust, slab_start, slab_planes, 1, total_y, total_z
    )
    for step_index in range(STEPS):
        extended = with_halo(velocity, (("space", 1),), 1)
        start_plane = slab_start - 1
        length = extended.shape[1]
        global_x = start_plane + jnp.arange(length, dtype=jnp.int32)
        inside = jnp.clip(last_plane - start_plane, 0, length - 1)
        edge_plane = lax.dynamic_index_in_dim(extended, inside, axis=1, keepdims=True)
        below_mask = (global_x < 0)[None, :, None, None]
        above_mask = (global_x > last_plane)[None, :, None, None]
        velocity = advance(
            jnp.where(
                below_mask, fine_inflow[:, None], jnp.where(above_mask, edge_plane, extended)
            ),
            fine_inflow,
            fine_drag,
        )
    coarse_planes = slab_planes * spaces // 8
    coarse_drag = drag_field(
        turbine_x, turbine_y, turbine_z, thrust, 0, coarse_planes, 8, coarse_y, coarse_z
    )
    partner_inflow = 1.0 + AMPLITUDE * restrict(fine_noise)
    alone_inflow = 1.0 + AMPLITUDE * alone_noise
    partner = run_whole(
        partner_state.reshape(pair_count, coarse_planes, coarse_y, coarse_z),
        partner_inflow,
        coarse_drag,
    )
    alone_runs = run_whole(
        coarse_state.reshape(-1, coarse_planes, coarse_y, coarse_z), alone_inflow, coarse_drag
    )
    fine_power = jnp.sum(fine_drag * velocity * velocity * velocity, axis=(1, 2, 3)) / 256.0
    partner_power = jnp.sum(coarse_drag * partner * partner * partner, axis=(1, 2, 3)) / 4.0
    alone_power = jnp.sum(coarse_drag * alone_runs * alone_runs * alone_runs, axis=(1, 2, 3)) / 4.0
    leader = (slab_index == 0).astype(jnp.float32)
    partials = jnp.stack(
        [jnp.sum(fine_power) - leader * jnp.sum(partner_power), jnp.sum(alone_power)]
    )
    totals = lax.psum(partials, ("space", "sample"))
    samples_count = lax.axis_size("sample")
    counts = jnp.array(
        [pair_count * samples_count, alone_runs.shape[0] * spaces * samples_count], jnp.float32
    )
    estimate = totals / counts
    fine_field = velocity.reshape(pair_count, slab_planes, total_y * total_z)
    partner_field = partner.reshape(pair_count, coarse_planes, coarse_y * coarse_z)
    coarse_field = alone_runs.reshape(alone_runs.shape[0], coarse_planes, coarse_y * coarse_z)
    return (fine_field, partner_field, coarse_field, estimate)


def solution(mesh):
    placed = (
        P("sample", None, "space", None),
        P("sample", None),
        P("sample", "space", None),
        P("sample", None, None),
        P(("space", "sample"), None, None),
        P(),
        P(),
        P(),
        P(),
    )
    return jax.shard_map(
        shards,
        mesh=mesh,
        in_specs=placed,
        out_specs=(
            P("sample", "space", None),
            P("sample", None, None),
            P(("space", "sample"), None, None),
            P(),
        ),
        check_vma=False,
    )
```

profile of v0, /device:TPU:0, one launch (start us, length us, event | category | flops | bytes accessed | tf_op | source)
XLA Modules:
  0.0 247.3 jit_solution(2681329605193786550)
XLA Ops:
  13.2 2.0 convolution_bitcast_fusion.1
  15.3 1.6 reshape.827
  16.9 1.5 fusion.172
  18.5 3.3 %collective-permute-start = (f32[2,1,512,256]{3,2,1,0:T(8,128)}, f32[2,1,512,256]{3,2,1,0:T(8,128)}, u32[]{:S(2)}, u32[]{:S(2)}) collective-permute-start(f32[2,1,512,256]{3,2,1,0:T(8,128)} %get-tuple-element.29), channel_id=1, source_target_pairs={{0,2},{2,4},{4,6},{6,8},{8,10},{10,12},{12,14},{14,16},{16,18},{18... | collective-permute-start | bytes 3145736 | tf_op jit(solution)/shard_map/ppermute | solution.py:23
  21.8 1.3 collective-permute-start.1
  23.2 1.6 gather_fusion.1
  24.8 4.4 %convolution_bitcast_fusion = f32[16,32,512]{2,1,0:T(8,128)} fusion(f32[16,2,32,256]{3,2,1,0:T(8,128)} %gather_fusion.1, f32[1,256,512]{2,1,0:T(8,128)} %copy-done.9, f32[1,256,512]{2,1,0:T(8,128)} %copy-done.8, pred[16]{0:T(512)(128)(4,1)S(1)} %compare_and_fusion), kind=kOutput, calls=%fused_computation.42 | convolution fusion | flops 1611137024 | bytes 3145744 | tf_op jit(solution)/shard_map/ncks,csj->nkj/dot_general | solution.py:141
  29.3 8.4 %all-to-all-start = ((f32[16,32,512]{2,1,0:T(8,128)}), f32[16,32,512]{2,1,0:T(8,128)}, u32[]{:S(2)}, u32[]{:S(2)}) async-start(f32[16,32,512]{2,1,0:T(8,128)} %convolution_bitcast_fusion), calls=%async_computation | async-start | bytes 2097152 | tf_op jit(solution)/shard_map/all_to_all | solution.py:142
  42.3 5.0 %sine_negate_fusion = (f32[1,512,512]{1,2,0:T(8,128)}, f32[1,512,512]{1,2,0:T(8,128)}) fusion(), kind=kLoop, calls=%fused_computation.52 | loop fusion | flops 3932160 | bytes 2097152 | tf_op jit(solution)/shard_map/neg | solution.py:132
  52.2 7.8 %fusion = f32[2,512,256]{2,0,1:T(2,128)S(1)} fusion(f32[16]{0:T(128)S(1)} %copy-done.17, s32[16]{0:T(128)S(1)} %copy-done.22, s32[2]{0:T(128)S(1)} %iota_add_fusion, f32[2,8,512,256]{3,2,1,0:T(8,128)S(1)} %bitcast.72), kind=kOutput, calls=%fused_computation.2 | convolution fusion | flops 50331712 | bytes 9437320 | tf_op jit(solution)/shard_map/dot_general | solution.py:76
  60.1 1.5 broadcast_add_fusion
  61.6 61.0 %all-reduce.2.cloned.1.call-done = f32[2,512,256]{2,1,0:T(8,128)} async-done(((f32[2,512,256]{2,1,0:T(8,128)}), f32[2,512,256]{2,1,0:T(8,128)}) %all-reduce.2.cloned.1.call-update) | async-done | bytes 1048592 | tf_op jit(solution)/shard_map/psum | solution.py:140
  122.6 2.4 broadcast_multiply_fusion.1
  125.0 12.1 %reshape.818 = f32[2,64,8,32,8]{4,3,2,1,0:T(8,128)} reshape(f32[2,512,256]{2,1,0:T(8,128)} %get-tuple-element.30) | data formatting | bytes 2097152 | tf_op jit(solution)/shard_map/reshape | solution.py:83
  137.1 7.0 %reduce_sum.67 = f32[2,64,32]{2,1,0:T(8,128)S(1)} reduce(f32[2,64,8,32,8]{4,3,2,1,0:T(8,128)} %reshape.818, f32[]{:T(128)} %constant.168.clone.1), dimensions={2,4}, to_apply=%region_1.2 | reduce | flops 258048 | bytes 1064964 | tf_op jit(solution)/shard_map/reduce_sum | solution.py:83
  144.1 1.7 fusion.66
  149.3 1.3 constant_dynamic-update-slice_fusion.2
  150.8 1.3 constant_dynamic-update-slice_fusion
  154.8 2.8 %fusion.15 = f32[2,2,512,256]{3,2,1,0:T(8,128)S(1)} fusion(f32[2,4,512,256]{3,2,1,0:T(8,128)S(1)} %select_select_fusion.1, f32[2,2,511,256]{3,2,1,0:T(8,128)S(1)} %get-tuple-element.23, f32[2,2,1,256]{3,2,1,0:T(1,128)S(1)} %get-tuple-element.25, f32[2,2,1,256]{3,2,1,0:T(1,128)S(1)} %get-tuple-element.24, f32[2,2,511,256]{3,2,1,0:T(8,128)S(1)} %get-tuple-element.22, ...), kind=kLoop, calls=%fused_computation.24 | loop fusion | flops 12058624 | bytes 18874368 | tf_op jit(solution)/shard_map/div | solution.py:50
  157.6 1.5 fusion.171
  159.1 1.3 collective-permute-start.3
  160.4 4.0 %collective-permute-start.2 = (f32[2,1,512,256]{3,2,1,0:T(8,128)}, f32[2,1,512,256]{3,2,1,0:T(8,128)}, u32[]{:S(2)}, u32[]{:S(2)}) collective-permute-start(f32[2,1,512,256]{3,2,1,0:T(8,128)} %get-tuple-element.26), channel_id=1, source_target_pairs={{0,2},{2,4},{4,6},{6,8},{8,10},{10,12},{12,14},{14,16},{16,18},{18... | collective-permute-start | bytes 3145736 | tf_op jit(solution)/shard_map/ppermute | solution.py:23
  164.4 2.9 %reshape.822 = f32[512,2,256]{2,1,0:T(2,128)} reshape(f32[16,32,512]{2,1,0:T(8,128)} %all-to-all-done) | data formatting | bytes 2097152 | tf_op jit(solution)/shard_map/reshape.7
  167.3 4.5 %fusion.31 = f32[512,256]{1,0:T(8,128)} fusion(f32[1,512,512]{1,2,0:T(8,128)} %get-tuple-element.84, f32[1,512,512]{1,2,0:T(8,128)} %get-tuple-element.85, f32[512,2,256]{2,1,0:T(2,128)} %reshape.822), kind=kOutput, calls=%fused_computation.45 | convolution fusion | flops 1611268096 | bytes 3670016 | tf_op jit(solution)/shard_map/nkcz,cky->nyz/dot_general | solution.py:143
  171.8 7.1 %reshape.823 = f32[64,8,32,8]{3,2,1,0:T(8,128)} reshape(f32[512,256]{1,0:T(8,128)} %fusion.31) | data formatting | bytes 1048576 | tf_op jit(solution)/shard_map/reshape | solution.py:83
  178.9 4.1 %reduce_sum.68 = f32[64,32]{1,0:T(8,128)S(1)} reduce(f32[64,8,32,8]{3,2,1,0:T(8,128)} %reshape.823, f32[]{:T(128)} %constant.168.clone.1), dimensions={1,3}, to_apply=%region_2.3 | reduce | flops 129024 | bytes 532484 | tf_op jit(solution)/shard_map/reduce_sum | solution.py:83
  183.0 1.4 fusion.100
  186.8 2.0 pad_maximum_fusion
  188.9 2.1 select_select_fusion
  193.7 3.2 %fusion.3 = (f32[2]{0:T(128)S(1)}, f32[2,2,512,256]{3,2,1,0:T(8,128)S(1)}) fusion(f32[2,512,256]{2,1,0:T(8,128)S(1)} %copy-done.10, f32[2,512,256]{2,1,0:T(8,128)S(1)} %copy-done.5, f32[2,512,256]{2,1,0:T(8,128)S(1)} %get-tuple-element.31, f32[2,2,512,1]{3,2,1,0:T(8,128)S(1)} %get-tuple-element.15, f32[2,2,512,255]{3,2,1,0:T(8,128)S(1)} %get-tuple-element.17, ...), kind=kLoop, calls=%fused_computation.10 | loop fusion | flops 14155774 | bytes 19922952 | tf_op jit(solution)/shard_map/reduce_sum | solution.py:184
  198.2 2.4 reshape.816
  200.6 39.4 %psum.15 = f32[2]{0:T(128)S(1)} all-reduce(f32[2]{0:T(128)S(1)} %pad_maximum_fusion.9), channel_id=1, replica_groups=mesh['space'=16,'sample'=2] {'space','sample'}, use_global_device_ids=true, to_apply=%region_8.9 | all-reduce | flops 2 | bytes 16 | tf_op jit(solution)/shard_map/psum | solution.py:191
  (132 shorter events, 26.8 us)
Async XLA Ops:
  7.2 3.8 %copy-start = (f32[18,2,32,256]{3,2,1,0:T(8,128)S(1)}, f32[18,2,32,256]{3,2,1,0:T(8,128)}, u32[]{:S(2)}) copy-start(f32[18,2,32,256]{3,2,1,0:T(8,128)} %param.10) | copy-start | bytes 3538948
  7.2 115.4 %all-reduce.2.cloned.1.call-start = ((), (), s32[]{:S(2)}) async-start(), calls=%async_computation.1 | async-start | bytes 2097152 | tf_op jit(solution)/shard_map/psum | solution.py:140
  11.6 1.6 copy-start.9
  16.9 6.2 %copy-start.23 = (s32[1,18]{1,0:T(1,128)S(1)}, s32[1,18]{1,0:T(1,128)}, u32[]{:S(2)}) copy-start(s32[1,18]{1,0:T(1,128)} %param.11) | copy-start | bytes 220
  18.5 130.8 %collective-permute-start = (f32[2,1,512,256]{3,2,1,0:T(8,128)}, f32[2,1,512,256]{3,2,1,0:T(8,128)}, u32[]{:S(2)}, u32[]{:S(2)}) collective-permute-start(f32[2,1,512,256]{3,2,1,0:T(8,128)} %get-tuple-element.29), channel_id=1, source_target_pairs={{0,2},{2,4},{4,6},{6,8},{8,10},{10,12},{12,14},{14,16},{16,18},{18... | collective-permute-start | bytes 3145736 | tf_op jit(solution)/shard_map/ppermute | solution.py:23
  21.8 129.0 %collective-permute-start.1 = (f32[2,1,512,256]{3,2,1,0:T(8,128)}, f32[2,1,512,256]{3,2,1,0:T(8,128)}, u32[]{:S(2)}, u32[]{:S(2)}) collective-permute-start(f32[2,1,512,256]{3,2,1,0:T(8,128)} %get-tuple-element.28), channel_id=1, source_target_pairs={{2,0},{4,2},{6,4},{8,6},{10,8},{12,10},{14,12},{16,14},{18,16},{20... | collective-permute-start | bytes 3145736 | tf_op jit(solution)/shard_map/ppermute | solution.py:25
  24.8 12.8 %copy-start.15 = (f32[2,4,2048]{2,1,0:T(4,128)S(1)}, f32[2,4,2048]{2,1,0:T(4,128)}, u32[]{:S(2)}) copy-start(f32[2,4,2048]{2,1,0:T(4,128)} %param.13) | copy-start | bytes 196612
  29.3 135.2 %all-to-all-start = ((f32[16,32,512]{2,1,0:T(8,128)}), f32[16,32,512]{2,1,0:T(8,128)}, u32[]{:S(2)}, u32[]{:S(2)}) async-start(f32[16,32,512]{2,1,0:T(8,128)} %convolution_bitcast_fusion), calls=%async_computation | async-start | bytes 2097152 | tf_op jit(solution)/shard_map/all_to_all | solution.py:142
  37.6 2.8 %copy-start.20 = (s32[16]{0:T(128)S(1)}, s32[16]{0:T(128)}, u32[]{:S(2)}) copy-start(s32[16]{0:T(128)} %param.17) | copy-start | bytes 196
  37.6 2.8 %copy-start.21 = (s32[16]{0:T(128)S(1)}, s32[16]{0:T(128)}, u32[]{:S(2)}) copy-start(s32[16]{0:T(128)} %param.16) | copy-start | bytes 196
  37.8 3.2 %copy-start.2 = (f32[2,4,64,32]{3,2,1,0:T(8,128)}, f32[2,4,64,32]{3,2,1,0:T(8,128)S(1)}, u32[]{:S(2)}) copy-start(f32[2,4,64,32]{3,2,1,0:T(8,128)S(1)} %reshape.817) | copy-start | bytes 196612
  37.8 3.2 %copy-start.22 = (s32[16]{0:T(128)S(1)}, s32[16]{0:T(128)}, u32[]{:S(2)}) copy-start(s32[16]{0:T(128)} %param.15) | copy-start | bytes 196
  37.8 3.3 %copy-start.17 = (f32[16]{0:T(128)S(1)}, f32[16]{0:T(128)}, u32[]{:S(2)}) copy-start(f32[16]{0:T(128)} %param.18) | copy-start | bytes 196
  40.4 6.9 %copy-start.16 = (f32[1,4,2048]{2,1,0:T(4,128)S(1)}, f32[1,4,2048]{2,1,0:T(4,128)}, u32[]{:S(2)}) copy-start(f32[1,4,2048]{2,1,0:T(4,128)} %param.14) | copy-start | bytes 98308
  41.5 9.3 %copy-start.13 = (f32[4,64,32]{2,1,0:T(8,128)}, f32[4,64,32]{2,1,0:T(8,128)S(1)}, u32[]{:S(2)}) copy-start(f32[4,64,32]{2,1,0:T(8,128)S(1)} %reshape.819) | copy-start | bytes 98308
  47.4 12.7 %copy-start.6 = (f32[1,4,64,32]{3,2,1,0:T(8,128)}, f32[1,4,64,32]{3,2,1,0:T(8,128)S(1)}, u32[]{:S(2)}) copy-start(f32[1,4,64,32]{3,2,1,0:T(8,128)S(1)} %reshape.821) | copy-start | bytes 98308
  137.0 7.1 %copy-start.3 = (f32[2,4,64,32]{3,2,1,0:T(8,128)S(1)}, f32[2,4,64,32]{3,2,1,0:T(8,128)}, u32[]{:S(2)}) copy-start(f32[2,4,64,32]{3,2,1,0:T(8,128)} %copy-done.2) | copy-start | bytes 196612
  137.0 7.1 %slice-start = ((f32[2,4,64,32]{3,2,1,0:T(8,128)}), f32[2,1,64,32]{3,2,1,0:T(8,128)S(1)}, s32[]{:S(2)}) async-start(f32[2,4,64,32]{3,2,1,0:T(8,128)} %copy-done.2), calls=%async_computation.2 | async-start | bytes 131072 | tf_op jit(solution)/shard_map/slice | solution.py:89
  145.8 0.9 copy-start.12
  145.9 1.0 copy-start.14
  150.8 1.4 copy-start.18
  150.8 1.4 copy-start.19
  153.6 1.2 copy-start.4
  159.1 27.7 %collective-permute-start.3 = (f32[2,1,512,256]{3,2,1,0:T(8,128)}, f32[2,1,512,256]{3,2,1,0:T(8,128)}, u32[]{:S(2)}, u32[]{:S(2)}) collective-permute-start(f32[2,1,512,256]{3,2,1,0:T(8,128)} %get-tuple-element.27), channel_id=1, source_target_pairs={{2,0},{4,2},{6,4},{8,6},{10,8},{12,10},{14,12},{16,14},{18,16},{20... | collective-permute-start | bytes 3145736 | tf_op jit(solution)/shard_map/ppermute | solution.py:25
  160.4 26.4 %collective-permute-start.2 = (f32[2,1,512,256]{3,2,1,0:T(8,128)}, f32[2,1,512,256]{3,2,1,0:T(8,128)}, u32[]{:S(2)}, u32[]{:S(2)}) collective-permute-start(f32[2,1,512,256]{3,2,1,0:T(8,128)} %get-tuple-element.26), channel_id=1, source_target_pairs={{0,2},{2,4},{4,6},{6,8},{8,10},{10,12},{12,14},{14,16},{16,18},{18... | collective-permute-start | bytes 3145736 | tf_op jit(solution)/shard_map/ppermute | solution.py:23
  178.8 4.1 %copy-start.7 = (f32[1,4,64,32]{3,2,1,0:T(8,128)S(1)}, f32[1,4,64,32]{3,2,1,0:T(8,128)}, u32[]{:S(2)}) copy-start(f32[1,4,64,32]{3,2,1,0:T(8,128)} %copy-done.6) | copy-start | bytes 98308
  178.8 4.1 %slice-start.1 = ((f32[1,4,64,32]{3,2,1,0:T(8,128)}), f32[1,1,64,32]{3,2,1,0:T(8,128)S(1)}, s32[]{:S(2)}) async-start(f32[1,4,64,32]{3,2,1,0:T(8,128)} %copy-done.6), calls=%async_computation.3 | async-start | bytes 65536 | tf_op jit(solution)/shard_map/slice | solution.py:89
  178.9 4.1 %copy-start.11 = (f32[1,4,64,32]{3,2,1,0:T(8,128)S(1)}, f32[1,4,64,32]{3,2,1,0:T(8,128)}, u32[]{:S(2)}) copy-start(f32[1,4,64,32]{3,2,1,0:T(8,128)} %reshape.824) | copy-start | bytes 98308
  192.1 1.2 copy-start.5
  192.1 1.5 copy-start.10
  198.2 42.3 %copy-start.1 = (f32[18,2,32,256]{3,2,1,0:T(8,128)S(1)}, f32[18,2,32,256]{3,2,1,0:T(8,128)}, u32[]{:S(2)}) copy-start(f32[18,2,32,256]{3,2,1,0:T(8,128)} %param.10) | copy-start | bytes 3538948
  198.2 41.8 %copy-start.24 = (f32[2]{0:T(128)S(1)}, f32[2]{0:T(128)}, u32[]{:S(2)}) copy-start(f32[2]{0:T(128)} %constant.181) | copy-start | bytes 28
  (1 other events, 0.8 us)
Sparse Core Ops, SparseCore 0:
  15.4 107.1 all-reduce.1
where the time goes:
time: 248 us; the launch traced here: 247 us
  waiting for transfers between devices  61 us (25%)
  local copies, waits for them, and re-layouts  48.3 us (19%)
  other arithmetic  43.8 us (18%)
  blocking collectives  39.4 us (16%)
  matrix products  19.8 us (8%)
  starting transfers between devices  18.3 us (7%)
  between operations  16.6 us (7%)
    psum x1, waiting for transfers between devices, shards(): fine_noise = lax.psum(partial_noise, 'space') * norm_scale  61 us
    psum x1, blocking collectives, shards(): totals = lax.psum(partials, ('space', 'sample'))  39.4 us
    reshape x2, local copies, waits for them, and re-layouts, restrict(): values.reshape(leading + (y_count // 8, 8, z_count // 8, 8))  19.2 us
    reduce_sum x2, other arithmetic, restrict(): values.reshape(leading + (y_count // 8, 8, z_count // 8, 8))  11.1 us
    all_to_all x1, starting transfers between devices, shards(): lax.all_to_all(alone_pq, 'space', split_axis=0, concat_axis=1, tiled=True)  8.37 us
    dot_general x2, matrix products, drag_field(): jnp.dot(along_x.T, cross_mask, precision=HIGHEST)  8.14 us
    ppermute x2, starting transfers between devices, with_halo(): lax.ppermute(tail, axis, [(i, (i + 1) % count) for i in range(ends)])  7.36 us
    div x3, other arithmetic, advance(): return updated / (1.0 + resistance)  5.88 us
  transfers between devices with their start and end apart: 6, of which 1 were waited for; matrix products, arithmetic and copies ran while one was open for 36% of the time, Pallas kernels for 0%

commit v1 on v0

--- a/solution.py
+++ b/solution.py
@@ -3,6 +3,7 @@
 import jax.numpy as jnp
 from jax import lax
 from jax.sharding import PartitionSpec as P
+from jax.lax import all_gather
 
 STEPS = 2
 ADVECT = 0.3
@@ -137,7 +138,7 @@
     cosine_own, sine_own = twiddle(own_ky, y_cells, total_y)
     y_own = jnp.stack([cosine_own, -sine_own])
     partial_noise = jnp.einsum("nkcz,cky->nyz", pair_pq, y_own, precision=HIGHEST)
-    fine_noise = lax.psum(partial_noise, "space") * norm_scale
+    fine_noise = jnp.sum(all_gather(partial_noise, "space"), axis=0) * norm_scale
     alone_pq = jnp.einsum("ncks,csj->nkj", alone_spectra, z_table, precision=HIGHEST)
     gathered_pq = lax.all_to_all(alone_pq, "space", split_axis=0, concat_axis=1, tiled=True)
     full_plane = jnp.einsum(

time: 248 us -> 306 us (1.23)
  blocking collectives: 39.4 us -> 57.7 us
  waiting for transfers between devices: 61 us -> 76.7 us
  other arithmetic: 43.8 us -> 56 us
  local copies, waits for them, and re-layouts: 48.3 us -> 56.7 us
    psum x1 -> x0, waiting for transfers between devices: 61 us -> none  [shards(): fine_noise = lax.psum(partial_noise, 'space') * norm_scale]
    all_gather x0 -> x1, waiting for transfers between devices: none -> 58.5 us  [shards(): all_gather(partial_noise, 'space')]
    psum x1, blocking collectives: 39.4 us -> 57.7 us  [shards(): totals = lax.psum(partials, ('space', 'sample'))]
    all_to_all x1, waiting for transfers between devices: 0.01 us -> 18.2 us  [shards(): lax.all_to_all(alone_pq, 'space', split_axis=0, concat_axis=1, tiled=True)]
    reshape x2 -> x1, local copies, waits for them, and re-layouts: 19.2 us -> 7.08 us  [restrict(): values.reshape(leading + (y_count // 8, 8, z_count // 8, 8))]
    mul x0 -> x1, local copies, waits for them, and re-layouts: none -> 11.1 us  [shards(): jnp.sum(all_gather(partial_noise, 'space'), axis=0) * norm_scale]
    reduce_sum x0 -> x1, other arithmetic: none -> 6.98 us  [shards(): jnp.sum(all_gather(partial_noise, 'space'), axis=0) * norm_scale]
    dot_general x2, matrix products: 8.14 us -> 12.7 us  [drag_field(): jnp.dot(along_x.T, cross_mask, precision=HIGHEST)]
  transfers between devices with their start and end apart: 6 -> 6, of which waited for: 1 -> 2; matrix products, arithmetic and copies ran while one was open for 36% -> 21% of each run, Pallas kernels for 0% -> 0%
where the time goes in v1:
time: 306 us; the launch traced here: 305 us
  waiting for transfers between devices  76.7 us (25%)
  blocking collectives  57.7 us (19%)
  local copies, waits for them, and re-layouts  56.7 us (19%)
  other arithmetic  56 us (18%)
  matrix products  22.8 us (7%)
  starting transfers between devices  18.6 us (6%)
  between operations  16.9 us (6%)
    all_gather x1, waiting for transfers between devices, shards(): all_gather(partial_noise, 'space')  58.5 us
    psum x1, blocking collectives, shards(): totals = lax.psum(partials, ('space', 'sample'))  57.7 us
    all_to_all x1, waiting for transfers between devices, shards(): lax.all_to_all(alone_pq, 'space', split_axis=0, concat_axis=1, tiled=True)  18.2 us
    dot_general x2, matrix products, drag_field(): jnp.dot(along_x.T, cross_mask, precision=HIGHEST)  12.7 us
    reduce_sum x2, other arithmetic, restrict(): values.reshape(leading + (y_count // 8, 8, z_count // 8, 8))  11.3 us
    mul x1, local copies, waits for them, and re-layouts, shards(): jnp.sum(all_gather(partial_noise, 'space'), axis=0) * norm_scale  11.1 us
    all_to_all x1, starting transfers between devices, shards(): lax.all_to_all(alone_pq, 'space', split_axis=0, concat_axis=1, tiled=True)  8.49 us
    unnamed x86, local copies, waits for them, and re-layouts  7.89 us
  transfers between devices with their start and end apart: 6, of which 2 were waited for; matrix products, arithmetic and copies ran while one was open for 21% of the time, Pallas kernels for 0%

profile of v1, /device:TPU:0, one launch (start us, length us, event | category | flops | bytes accessed | tf_op | source)
XLA Modules:
  0.0 305.4 jit_solution(9534023889358913570)
XLA Ops:
  13.2 2.0 convolution_bitcast_fusion.1
  15.3 1.6 reshape.830
  18.4 3.4 %collective-permute-start = (f32[2,1,512,256]{3,2,1,0:T(8,128)}, f32[2,1,512,256]{3,2,1,0:T(8,128)}, u32[]{:S(2)}, u32[]{:S(2)}) collective-permute-start(f32[2,1,512,256]{3,2,1,0:T(8,128)} %get-tuple-element.29), channel_id=1, source_target_pairs={{0,2},{2,4},{4,6},{6,8},{8,10},{10,12},{12,14},{14,16},{16,18},{18... | collective-permute-start | bytes 3145736 | tf_op jit(solution)/shard_map/ppermute | solution.py:24
  23.2 1.6 gather_fusion.1
  24.8 4.7 %convolution_bitcast_fusion = f32[16,32,512]{2,1,0:T(8,128)} fusion(f32[16,2,32,256]{3,2,1,0:T(8,128)} %gather_fusion.1, f32[1,256,512]{2,1,0:T(8,128)} %copy-done.12, f32[1,256,512]{2,1,0:T(8,128)} %copy-done.11, pred[16]{0:T(512)(128)(4,1)S(1)} %compare_and_fusion), kind=kOutput, calls=%fused_computation.42 | convolution fusion | flops 1611137024 | bytes 3145744 | tf_op jit(solution)/shard_map/ncks,csj->nkj/dot_general | solution.py:142
  29.5 8.5 %all-to-all-start = ((f32[16,32,512]{2,1,0:T(8,128)}), f32[16,32,512]{2,1,0:T(8,128)}, u32[]{:S(2)}, u32[]{:S(2)}) async-start(f32[16,32,512]{2,1,0:T(8,128)} %convolution_bitcast_fusion), calls=%async_computation | async-start | bytes 2097152 | tf_op jit(solution)/shard_map/all_to_all | solution.py:143
  39.4 5.0 %sine_negate_fusion = (f32[1,512,512]{1,2,0:T(8,128)}, f32[1,512,512]{1,2,0:T(8,128)}) fusion(), kind=kLoop, calls=%fused_computation.52 | loop fusion | flops 3932160 | bytes 2097152 | tf_op jit(solution)/shard_map/neg | solution.py:133
  48.3 4.0 %broadcast_multiply_fusion = f32[16,512,256]{2,1,0:T(8,128)} fusion(f32[16,256]{1,0:T(8,128)S(1)} %fusion.130, f32[16,512]{1,0:T(8,128)S(1)} %fusion.128), kind=kLoop, calls=%fused_computation.7 | loop fusion | flops 2097152 | bytes 8437760 | tf_op jit(solution)/shard_map/mul | solution.py:74
  55.3 12.4 %fusion = f32[2,512,256]{2,0,1:T(2,128)S(1)} fusion(f32[16]{0:T(128)} %param.18, s32[16]{0:T(128)} %param.15, s32[2]{0:T(128)} %iota_add_fusion, f32[2,8,512,256]{3,2,1,0:T(8,128)} %bitcast.73), kind=kOutput, calls=%fused_computation.2 | convolution fusion | flops 50331712 | bytes 9437320 | tf_op jit(solution)/shard_map/dot_general | solution.py:77
  71.9 2.1 copy-done.7
  75.1 18.2 %all-to-all-done = f32[16,32,512]{2,1,0:T(8,128)} async-done(((f32[16,32,512]{2,1,0:T(8,128)}), f32[16,32,512]{2,1,0:T(8,128)}, u32[]{:S(2)}, u32[]{:S(2)}) %all-to-all-start) | async-done | bytes 1048608 | tf_op jit(solution)/shard_map/all_to_all | solution.py:143
  93.2 1.9 reshape.825
  95.1 2.6 fusion.31
  97.7 7.1 %reshape.826 = f32[64,8,32,8]{3,2,1,0:T(8,128)} reshape(f32[512,256]{1,0:T(8,128)} %fusion.31) | data formatting | bytes 1048576 | tf_op jit(solution)/shard_map/reshape | solution.py:84
  104.9 4.1 %reduce_sum.78 = f32[64,32]{1,0:T(8,128)S(1)} reduce(f32[64,8,32,8]{3,2,1,0:T(8,128)} %reshape.826, f32[]{:T(128)} %constant.159.clone.1), dimensions={1,3}, to_apply=%region_2.3 | reduce | flops 129024 | bytes 532484 | tf_op jit(solution)/shard_map/reduce_sum | solution.py:84
  111.7 58.5 %all-gather.3.cloned.1.call-done = f32[32,512,256]{2,1,0:T(8,128)} async-done(((f32[2,512,256]{2,1,0:T(8,128)}), f32[32,512,256]{2,1,0:T(8,128)}) %all-gather.3.cloned.1.call-update) | async-done | bytes 16777232 | tf_op jit(solution)/shard_map/all_gather | solution.py:141
  170.3 7.0 %reduce_sum.76 = f32[2,512,256]{2,1,0:T(8,128)S(1)} reduce(f32[16,2,512,256]{3,2,1,0:T(8,128)} %bitcast.74, f32[]{:T(128)} %constant.159.clone.1), dimensions={0}, to_apply=%region_0.1 | reduce | flops 3932160 | bytes 17825796 | tf_op jit(solution)/shard_map/reduce_sum | solution.py:141
  178.5 2.8 select_select_fusion.1
  181.3 2.5 fusion.169
  183.9 2.8 fusion.167
  186.6 1.7 fusion.168
  188.4 11.1 %mul.452 = f32[2,64,8,32,8]{4,3,2,1,0:T(8,128)} reshape(f32[2,512,256]{2,1,0:T(8,128)S(1)} %get-tuple-element.30) | data formatting | bytes 2097152 | tf_op jit(solution)/shard_map/mul | solution.py:141
  199.6 7.1 %reduce_sum.77 = f32[2,64,32]{2,1,0:T(8,128)S(1)} reduce(f32[2,64,8,32,8]{4,3,2,1,0:T(8,128)} %mul.452, f32[]{:T(128)} %constant.159.clone.1), dimensions={2,4}, to_apply=%region_1.2 | reduce | flops 258048 | bytes 1064964 | tf_op jit(solution)/shard_map/reduce_sum | solution.py:84
  208.6 6.5 %fusion.15 = f32[2,2,512,256]{3,2,1,0:T(8,128)S(1)} fusion(f32[2,4,512,256]{3,2,1,0:T(8,128)} %copy-done.2, f32[2,2,511,256]{3,2,1,0:T(8,128)} %get-tuple-element.23, f32[2,2,1,256]{3,2,1,0:T(1,128)S(1)} %get-tuple-element.25, f32[2,2,1,256]{3,2,1,0:T(1,128)S(1)} %get-tuple-element.24, f32[2,2,511,256]{3,2,1,0:T(8,128)S(1)} %copy-done.10, ...), kind=kLoop, calls=%fused_computation.24 | loop fusion | flops 12058624 | bytes 18874368 | tf_op jit(solution)/shard_map/div | solution.py:51
  215.2 1.5 fusion.171
  218.1 4.0 %collective-permute-start.2 = (f32[2,1,512,256]{3,2,1,0:T(8,128)}, f32[2,1,512,256]{3,2,1,0:T(8,128)}, u32[]{:S(2)}, u32[]{:S(2)}) collective-permute-start(f32[2,1,512,256]{3,2,1,0:T(8,128)} %get-tuple-element.26), channel_id=1, source_target_pairs={{0,2},{2,4},{4,6},{6,8},{8,10},{10,12},{12,14},{14,16},{16,18},{18... | collective-permute-start | bytes 3145736 | tf_op jit(solution)/shard_map/ppermute | solution.py:24
  223.4 1.7 reshape.823
  226.5 2.0 pad_maximum_fusion
  228.6 2.1 select_select_fusion
  233.4 3.2 %fusion.3 = (f32[2]{0:T(128)S(1)}, f32[2,2,512,256]{3,2,1,0:T(8,128)S(1)}) fusion(f32[2,512,256]{2,1,0:T(8,128)S(1)} %copy-done.13, f32[2,512,256]{2,1,0:T(8,128)S(1)} %copy-done.6, f32[2,512,256]{2,1,0:T(8,128)S(1)} %get-tuple-element.31, f32[2,2,512,1]{3,2,1,0:T(8,128)S(1)} %get-tuple-element.15, f32[2,2,512,255]{3,2,1,0:T(8,128)S(1)} %get-tuple-element.17, ...), kind=kLoop, calls=%fused_computation.10 | loop fusion | flops 14155774 | bytes 19922952 | tf_op jit(solution)/shard_map/reduce_sum | solution.py:185
  237.9 2.4 reshape.820
  240.3 57.7 %psum.7 = f32[2]{0:T(128)S(1)} all-reduce(f32[2]{0:T(128)S(1)} %pad_maximum_fusion.9), channel_id=1, replica_groups=mesh['space'=16,'sample'=2] {'space','sample'}, use_global_device_ids=true, to_apply=%region_8.9 | all-reduce | flops 2 | bytes 16 | tf_op jit(solution)/shard_map/psum | solution.py:192
  (167 shorter events, 34.6 us)
Async XLA Ops:
  7.2 163.1 %all-gather.3.cloned.1.call-start = ((), (), s32[]{:S(2)}) async-start(), calls=%async_computation.1 | async-start | bytes 17825792 | tf_op jit(solution)/shard_map/all_gather | solution.py:141
  16.9 6.2 %copy-start.40 = (s32[1,18]{1,0:T(1,128)S(1)}, s32[1,18]{1,0:T(1,128)}, u32[]{:S(2)}) copy-start(s32[1,18]{1,0:T(1,128)} %param.11) | copy-start | bytes 220
  18.4 50.7 %collective-permute-start = (f32[2,1,512,256]{3,2,1,0:T(8,128)}, f32[2,1,512,256]{3,2,1,0:T(8,128)}, u32[]{:S(2)}, u32[]{:S(2)}) collective-permute-start(f32[2,1,512,256]{3,2,1,0:T(8,128)} %get-tuple-element.29), channel_id=1, source_target_pairs={{0,2},{2,4},{4,6},{6,8},{8,10},{10,12},{12,14},{14,16},{16,18},{18... | collective-permute-start | bytes 3145736 | tf_op jit(solution)/shard_map/ppermute | solution.py:24
  21.8 48.8 %collective-permute-start.1 = (f32[2,1,512,256]{3,2,1,0:T(8,128)}, f32[2,1,512,256]{3,2,1,0:T(8,128)}, u32[]{:S(2)}, u32[]{:S(2)}) collective-permute-start(f32[2,1,512,256]{3,2,1,0:T(8,128)} %get-tuple-element.28), channel_id=1, source_target_pairs={{2,0},{4,2},{6,4},{8,6},{10,8},{12,10},{14,12},{16,14},{18,16},{20... | collective-permute-start | bytes 3145736 | tf_op jit(solution)/shard_map/ppermute | solution.py:26
  24.8 13.2 %copy-start.37 = (s32[16]{0:T(128)S(1)}, s32[16]{0:T(128)}, u32[]{:S(2)}) copy-start(s32[16]{0:T(128)} %param.17) | copy-start | bytes 196
  24.8 13.2 %copy-start.38 = (s32[16]{0:T(128)S(1)}, s32[16]{0:T(128)}, u32[]{:S(2)}) copy-start(s32[16]{0:T(128)} %param.16) | copy-start | bytes 196
  29.5 9.2 %copy-start.39 = (s32[16]{0:T(128)S(1)}, s32[16]{0:T(128)}, u32[]{:S(2)}) copy-start(s32[16]{0:T(128)} %param.15) | copy-start | bytes 196
  29.5 9.2 %copy-start.34 = (f32[16]{0:T(128)S(1)}, f32[16]{0:T(128)}, u32[]{:S(2)}) copy-start(f32[16]{0:T(128)} %param.18) | copy-start | bytes 196
  29.5 9.6 %copy-start.32 = (f32[2,4,2048]{2,1,0:T(4,128)S(1)}, f32[2,4,2048]{2,1,0:T(4,128)}, u32[]{:S(2)}) copy-start(f32[2,4,2048]{2,1,0:T(4,128)} %param.13) | copy-start | bytes 196612
  29.5 9.8 %copy-start.33 = (f32[1,4,2048]{2,1,0:T(4,128)S(1)}, f32[1,4,2048]{2,1,0:T(4,128)}, u32[]{:S(2)}) copy-start(f32[1,4,2048]{2,1,0:T(4,128)} %param.14) | copy-start | bytes 98308
  29.5 63.7 %all-to-all-start = ((f32[16,32,512]{2,1,0:T(8,128)}), f32[16,32,512]{2,1,0:T(8,128)}, u32[]{:S(2)}, u32[]{:S(2)}) async-start(f32[16,32,512]{2,1,0:T(8,128)} %convolution_bitcast_fusion), calls=%async_computation | async-start | bytes 2097152 | tf_op jit(solution)/shard_map/all_to_all | solution.py:143
  39.1 8.4 %copy-start.18 = (f32[4,64,32]{2,1,0:T(8,128)}, f32[4,64,32]{2,1,0:T(8,128)S(1)}, u32[]{:S(2)}) copy-start(f32[4,64,32]{2,1,0:T(8,128)S(1)} %reshape.822) | copy-start | bytes 98308
  39.3 15.1 %copy-start.3 = (f32[2,4,64,32]{3,2,1,0:T(8,128)}, f32[2,4,64,32]{3,2,1,0:T(8,128)S(1)}, u32[]{:S(2)}) copy-start(f32[2,4,64,32]{3,2,1,0:T(8,128)S(1)} %reshape.821) | copy-start | bytes 196612
  39.4 15.0 %copy-start.8 = (f32[1,4,64,32]{3,2,1,0:T(8,128)}, f32[1,4,64,32]{3,2,1,0:T(8,128)S(1)}, u32[]{:S(2)}) copy-start(f32[1,4,64,32]{3,2,1,0:T(8,128)S(1)} %reshape.824) | copy-start | bytes 98308
  74.0 21.1 %copy-start.14 = (f32[1,512,512]{1,2,0:T(8,128)S(1)}, f32[1,512,512]{1,2,0:T(8,128)}, u32[]{:S(2)}) copy-start(f32[1,512,512]{1,2,0:T(8,128)} %get-tuple-element.84) | copy-start | bytes 3145732
  74.0 21.1 %copy-start.15 = (f32[1,512,512]{1,2,0:T(8,128)S(1)}, f32[1,512,512]{1,2,0:T(8,128)}, u32[]{:S(2)}) copy-start(f32[1,512,512]{1,2,0:T(8,128)} %get-tuple-element.85) | copy-start | bytes 3145732
  104.8 4.2 %copy-start.28 = (f32[1,4,64,31]{3,2,1,0:T(8,128)S(1)}, f32[1,4,64,31]{3,2,1,0:T(8,128)}, u32[]{:S(2)}) copy-start(f32[1,4,64,31]{3,2,1,0:T(8,128)} %get-tuple-element.60) | copy-start | bytes 95236
  181.3 5.3 %copy-start.2 = (f32[2,4,512,256]{3,2,1,0:T(8,128)}, f32[2,4,512,256]{3,2,1,0:T(8,128)S(1)}, u32[]{:S(2)}) copy-start(f32[2,4,512,256]{3,2,1,0:T(8,128)S(1)} %select_select_fusion.1) | copy-start | bytes 12582916
  199.5 7.2 %copy-start.4 = (f32[2,4,64,32]{3,2,1,0:T(8,128)S(1)}, f32[2,4,64,32]{3,2,1,0:T(8,128)}, u32[]{:S(2)}) copy-start(f32[2,4,64,32]{3,2,1,0:T(8,128)} %copy-done.3) | copy-start | bytes 196612
  199.5 7.3 %slice-start = ((f32[2,4,64,32]{3,2,1,0:T(8,128)}), f32[2,1,64,32]{3,2,1,0:T(8,128)S(1)}, s32[]{:S(2)}) async-start(f32[2,4,64,32]{3,2,1,0:T(8,128)} %copy-done.3), calls=%async_computation.2 | async-start | bytes 131072 | tf_op jit(solution)/shard_map/slice | solution.py:90
  199.5 7.3 %copy-start.17 = (f32[4,64,32]{2,1,0:T(8,128)S(1)}, f32[4,64,32]{2,1,0:T(8,128)}, u32[]{:S(2)}) copy-start(f32[4,64,32]{2,1,0:T(8,128)} %broadcast_add_fusion.1) | copy-start | bytes 98308
  199.5 7.3 %copy-start.20 = (f32[2,4,63,32]{3,2,1,0:T(8,128)S(1)}, f32[2,4,63,32]{3,2,1,0:T(8,128)}, u32[]{:S(2)}) copy-start(f32[2,4,63,32]{3,2,1,0:T(8,128)} %get-tuple-element.46) | copy-start | bytes 193540
  199.5 7.3 %copy-start.21 = (f32[2,4,63,32]{3,2,1,0:T(8,128)S(1)}, f32[2,4,63,32]{3,2,1,0:T(8,128)}, u32[]{:S(2)}) copy-start(f32[2,4,63,32]{3,2,1,0:T(8,128)} %get-tuple-element.47) | copy-start | bytes 193540
  199.5 7.3 %copy-start.22 = (f32[2,4,64,31]{3,2,1,0:T(8,128)S(1)}, f32[2,4,64,31]{3,2,1,0:T(8,128)}, u32[]{:S(2)}) copy-start(f32[2,4,64,31]{3,2,1,0:T(8,128)} %get-tuple-element.42) | copy-start | bytes 190468
  199.5 7.3 %copy-start.23 = (f32[2,4,64,31]{3,2,1,0:T(8,128)S(1)}, f32[2,4,64,31]{3,2,1,0:T(8,128)}, u32[]{:S(2)}) copy-start(f32[2,4,64,31]{3,2,1,0:T(8,128)} %get-tuple-element.43) | copy-start | bytes 190468
  199.6 7.3 %copy-start.24 = (f32[2,4,64,1]{3,2,1,0:T(8,128)S(1)}, f32[2,4,64,1]{3,2,1,0:T(8,128)}, u32[]{:S(2)}) copy-start(f32[2,4,64,1]{3,2,1,0:T(8,128)} %get-tuple-element.44) | copy-start | bytes 6148
  199.6 7.3 %copy-start.25 = (f32[2,4,64,1]{3,2,1,0:T(8,128)S(1)}, f32[2,4,64,1]{3,2,1,0:T(8,128)}, u32[]{:S(2)}) copy-start(f32[2,4,64,1]{3,2,1,0:T(8,128)} %get-tuple-element.45) | copy-start | bytes 6148
  216.7 5.6 %copy-start.19 = (f32[4,64,32]{2,1,0:T(8,128)S(1)}, f32[4,64,32]{2,1,0:T(8,128)}, u32[]{:S(2)}) copy-start(f32[4,64,32]{2,1,0:T(8,128)} %copy-done.18) | copy-start | bytes 98308
  216.7 9.8 %collective-permute-start.3 = (f32[2,1,512,256]{3,2,1,0:T(8,128)}, f32[2,1,512,256]{3,2,1,0:T(8,128)}, u32[]{:S(2)}, u32[]{:S(2)}) collective-permute-start(f32[2,1,512,256]{3,2,1,0:T(8,128)} %get-tuple-element.27), channel_id=1, source_target_pairs={{2,0},{4,2},{6,4},{8,6},{10,8},{12,10},{14,12},{16,14},{18,16},{20... | collective-permute-start | bytes 3145736 | tf_op jit(solution)/shard_map/ppermute | solution.py:26
  218.1 8.4 %collective-permute-start.2 = (f32[2,1,512,256]{3,2,1,0:T(8,128)}, f32[2,1,512,256]{3,2,1,0:T(8,128)}, u32[]{:S(2)}, u32[]{:S(2)}) collective-permute-start(f32[2,1,512,256]{3,2,1,0:T(8,128)} %get-tuple-element.26), channel_id=1, source_target_pairs={{0,2},{2,4},{4,6},{6,8},{8,10},{10,12},{12,14},{14,16},{16,18},{18... | collective-permute-start | bytes 3145736 | tf_op jit(solution)/shard_map/ppermute | solution.py:24
  237.9 60.6 %copy-start.1 = (f32[18,2,32,256]{3,2,1,0:T(8,128)S(1)}, f32[18,2,32,256]{3,2,1,0:T(8,128)}, u32[]{:S(2)}) copy-start(f32[18,2,32,256]{3,2,1,0:T(8,128)} %param.10) | copy-start | bytes 3538948
  237.9 60.1 %copy-start.41 = (f32[2]{0:T(128)S(1)}, f32[2]{0:T(128)}, u32[]{:S(2)}) copy-start(f32[2]{0:T(128)} %constant.181) | copy-start | bytes 28
  (18 other events, 47.3 us)
Sparse Core Ops, SparseCore 0:
  15.4 154.8 all-gather.2
